TPU v7x, 32 devices: a whole 2x2x4 slice. The times are simulated.
32 devices in a mesh: rep: 2 (over y), seq: 8 (over z, x), grp: 2 (over core).
Axes of the slice: x: 2, y: 2, z: 4, core: 2. Of those that a mesh axis runs over, the one named last changes fastest.
Arguments:
- hidden: bfloat16 [4352, 8192], P(('rep', 'seq'), 'grp'), parts along dimension 0, may hold values from -6 to 6
- proj: bfloat16 [3, 256, 8192], P(None, 'seq', 'grp'), may hold values from -0.0625 to 0.0625
- short_taps: float32 [3, 3, 256], P(None, None, 'grp'), may hold values from -4 to 4
- filters: float32 [16, 128], P('grp'), may hold values from -0.5 to 0.5
- grad_out: bfloat16 [4352, 256], P(('rep', 'seq'), 'grp'), parts along dimension 0, may hold values from -6 to 6
- var_pos: int32 [256], P(('rep', 'seq')), parts along dimension 0, may hold values from 0 to 2175, as said below
- alt_hidden: bfloat16 [256, 8192], P(('rep', 'seq'), 'grp'), parts along dimension 0, may hold values from -6 to 6
Outputs:
- attribution: float32 [4352], P(('rep', 'seq')), parts along dimension 0
- effect: float32 [256], P(('rep', 'seq')), parts along dimension 0
There are 2 independent parts, one for each index of `rep`. A program takes and returns all parts, laid end to end along the dimension named above; an argument that names none is the same for every part. Nothing has to cross between parts.
Inputs may be any that keep to these rules, and one draw needn't show every extreme that they name: `var_pos`: variants v of block j (j * 16 <= v < (j + 1) * 16) lie in tokens j * 272 to (j + 1) * 272 - 1; each block holds the first and the last of those tokens.
All inputs are finite; a program needn't handle non-finite values.
Results may differ from a plain program's by a relative error of at most 0.0028.
Values may be sent and summed in bfloat16 or wider, within the bound.
No kernel may reach another device: no remote copies, remote signals or barrier semaphores. Data moves between devices by JAX's collectives and lax.ppermute only.
A program may use at most 64 MiB of HBM per device.

v0:
```python
import jax
import jax.numpy as jnp
from jax import lax
from jax.sharding import PartitionSpec as P

D = 8192
GROUP = 16


def shifted(block, axis, distance):
    devices = range(lax.axis_size(axis))
    route = [(i - distance, i) for i in devices if i - distance in devices]
    return lax.ppermute(block, axis, route)


def causal_taps(source, taps, leading):
    tap_count = taps.shape[0]
    row_count = source.shape[0]
    extended = jnp.concatenate([leading, source], 0)
    summed = jnp.zeros(source.shape, jnp.float32)
    for offset in range(tap_count):
        begin = tap_count - 1 - offset
        summed = summed + taps[offset] * extended[begin : begin + row_count]
    return summed


def later_taps(source, taps, trailing):
    tap_count = taps.shape[0]
    row_count = source.shape[0]
    extended = jnp.concatenate([source, trailing], 0)
    summed = jnp.zeros(source.shape, jnp.float32)
    for offset in range(tap_count):
        summed = summed + taps[offset] * extended[offset : offset + row_count]
    return summed


def long_filter(extended, filters, row_count, later):
    filter_span = filters.shape[1]
    per_channel = jnp.repeat(filters, GROUP, axis=0).T

    def accumulate(block, summed):
        for inner in range(8):
            offset = block * 8 + inner
            begin = offset if later else filter_span - 1 - offset
            section = lax.dynamic_slice_in_dim(extended, begin, row_count, 0)
            summed = (
                summed + lax.dynamic_index_in_dim(per_channel, offset, 0, keepdims=False) * section
            )
        return summed

    return lax.fori_loop(
        0, filter_span // 8, accumulate, jnp.zeros((row_count, extended.shape[1]), jnp.float32)
    )


def per_device(hidden, proj, short_taps, filters, grad_out, var_pos, alt_hidden):
    row_count = hidden.shape[0]
    tap_count = short_taps.shape[0]
    filter_span = filters.shape[1]
    partial_feature = jnp.einsum(
        "td,fcd->tfc",
        hidden,
        lax.all_gather(proj, "seq", axis=1, tiled=True),
        preferred_element_type=jnp.float32,
    )
    feature = lax.psum_scatter(partial_feature, "grp", scatter_dimension=2, tiled=True)
    short_rim = shifted(feature[row_count - tap_count + 1 :], "seq", 1)
    mixed = causal_taps(feature, short_taps, short_rim)
    product = mixed[:, 1] * mixed[:, 2]
    prior_product = shifted(product[row_count - filter_span + 1 :], "seq", 1)
    queries = mixed[:, 0]
    filtered = long_filter(jnp.concatenate([prior_product, product], 0), filters, row_count, False)
    upstream = grad_out.astype(jnp.float32)
    back_queries = upstream * filtered
    back_filtered = upstream * queries
    next_filtered = shifted(back_filtered[: filter_span - 1], "seq", -1)
    back_product = long_filter(
        jnp.concatenate([back_filtered, next_filtered], 0), filters, row_count, True
    )
    back_mixed = jnp.stack(
        [back_queries, back_product * mixed[:, 2], back_product * mixed[:, 1]], 1
    )
    next_mixed = shifted(back_mixed[: tap_count - 1], "seq", -1)
    back_feature = later_taps(back_mixed, short_taps, next_mixed).astype(jnp.bfloat16)
    all_channels = lax.all_gather(back_feature, "grp", axis=2, tiled=True)
    panels_again = lax.all_gather(proj, "seq", axis=1, tiled=True)
    back_hidden = jnp.einsum(
        "tfc,fcd->td", all_channels, panels_again, preferred_element_type=jnp.float32
    )
    hidden_float = hidden.astype(jnp.float32)
    attribution_part = jnp.sum(back_hidden * hidden_float, 1)
    local_rows = var_pos - lax.axis_index("seq") * row_count
    picked = jnp.take(back_hidden, local_rows, axis=0)
    present = jnp.take(hidden_float, local_rows, axis=0)
    change = alt_hidden.astype(jnp.float32) - present
    effect_part = jnp.sum(picked * change, 1)
    attribution, effect = lax.psum((attribution_part, effect_part), "grp")
    factor = D ** (-0.5)
    return (attribution * factor, effect * factor)


def solution(mesh):
    in_specs = (
        P(("rep", "seq"), "grp"),
        P(None, "seq", "grp"),
        P(None, None, "grp"),
        P("grp", None),
        P(("rep", "seq"), "grp"),
        P(("rep", "seq")),
        P(("rep", "seq"), "grp"),
    )
    out_specs = (P(("rep", "seq")), P(("rep", "seq")))
    return jax.shard_map(
        per_device, mesh=mesh, in_specs=in_specs, out_specs=out_specs, check_vma=False
    )
```

profile of v0, /device:TPU:9, one launch (start us, length us, event | category | flops | bytes accessed | tf_op | source)
XLA Modules:
  0.0 182.6 jit_solution(11757446988338695483)
XLA Ops:
  7.2 0.7 all-gather.2.cloned.1.call-update
  8.0 100.1 %all-gather.2.cloned.1.call-done = bf16[3,256,4096]{2,1,0:T(8,128)(2,1)} async-done(((bf16[3,32,4096]{2,1,0:T(8,128)(2,1)}), bf16[3,256,4096]{2,1,0:T(8,128)(2,1)}) %all-gather.2.cloned.1.call-update) | async-done | bytes 6291472 | tf_op jit(solution)/shard_map/all_gather | solution.py:63
  108.1 6.3 %fusion.30 = f32[272,3,256]{2,0,1:T(8,128)} fusion(bf16[3,256,4096]{2,1,0:T(8,128)(2,1)} %all-gather.2.cloned.1.call-done, bf16[272,4096]{1,0:T(8,128)(2,1)} %param.13), kind=kOutput, calls=%fused_computation.52 | convolution fusion | flops 1711276032 | bytes 9355264 | tf_op jit(solution)/shard_map/td,fcd->tfc/dot_general | solution.py:60
  114.5 9.7 %reduce-scatter.2.cloned.1.call-done = f32[272,3,128]{2,0,1:T(8,128)} async-done(((f32[272,3,256]{2,0,1:T(8,128)}), f32[272,3,128]{2,0,1:T(8,128)}) %reduce-scatter.2.cloned.1.call-update) | async-done | bytes 417808 | tf_op jit(solution)/shard_map/reduce_scatter | solution.py:66
  124.1 0.7 slice.65
  124.9 3.1 %collective-permute-start = (f32[2,3,128]{2,0,1:T(2,128)S(1)}, f32[2,3,128]{2,0,1:T(2,128)S(1)}, u32[]{:S(2)}, u32[]{:S(2)}) collective-permute-start(f32[2,3,128]{2,0,1:T(2,128)S(1)} %slice.65), channel_id=1, source_target_pairs={{0,2},{2,4},{4,6},{6,8},{8,10},{10,12},{12,14},{1,3},{3,5},{5,7},{... | collective-permute-start | bytes 9224 | tf_op jit(solution)/shard_map/ppermute | solution.py:13
  127.9 2.1 %collective-permute-done = f32[2,3,128]{2,0,1:T(2,128)S(1)} collective-permute-done((f32[2,3,128]{2,0,1:T(2,128)S(1)}, f32[2,3,128]{2,0,1:T(2,128)S(1)}, u32[]{:S(2)}, u32[]{:S(2)}) %collective-permute-start) | collective-permute-done | bytes 3104 | tf_op jit(solution)/shard_map/ppermute | solution.py:13
  130.1 1.5 fusion.35
  131.7 2.2 %collective-permute-start.2 = (f32[127,128]{1,0:T(8,128)S(1)}, f32[127,128]{1,0:T(8,128)S(1)}, u32[]{:S(2)}, u32[]{:S(2)}) collective-permute-start(f32[127,128]{1,0:T(8,128)S(1)} %slice.72), channel_id=1, source_target_pairs={{2,0},{4,2},{6,4},{8,6},{10,8},{12,10},{14,12},{3,1},{5,3},{7,5},{... | collective-permute-start | bytes 195080 | tf_op jit(solution)/shard_map/ppermute | solution.py:13
  134.0 3.1 %collective-permute-start.1 = (f32[127,128]{1,0:T(8,128)S(1)}, f32[127,128]{1,0:T(8,128)S(1)}, u32[]{:S(2)}, u32[]{:S(2)}) collective-permute-start(f32[127,128]{1,0:T(8,128)S(1)} %slice.70), channel_id=1, source_target_pairs={{0,2},{2,4},{4,6},{6,8},{8,10},{10,12},{12,14},{1,3},{3,5},{5,7},{... | collective-permute-start | bytes 195080 | tf_op jit(solution)/shard_map/ppermute | solution.py:13
  137.2 5.7 %while.34 = (s32[]{:T(128)}, f32[272,128]{1,0:T(8,128)S(1)}, f32[128,128]{1,0:T(8,128)S(1)}, f32[399,128]{1,0:T(8,128)S(1)}, s32[]{:T(128)}, /*index=5*/s32[]{:T...) while((s32[]{:T(128)}, f32[272,128]{1,0:T(8,128)S(1)}, ...), condition=%wide.region_4.5_spmd.clone, body=%wide.region_3.4_spmd.clone.sunk | while | flops 591923 | bytes 1405823 | solution.py:51
  138.1 0.2 fusion.54
  139.1 0.2 fusion.54
  139.5 0.2 fusion.54
  140.9 0.2 fusion.54
  142.0 0.2 fusion.54
  142.3 0.2 fusion.54
  143.0 5.8 %while.33 = (s32[]{:T(128)}, f32[272,128]{1,0:T(8,128)S(1)}, f32[128,128]{1,0:T(8,128)S(1)}, f32[399,128]{1,0:T(8,128)S(1)}, s32[]{:T(128)}, /*index=5*/s32[]{:T...) while((s32[]{:T(128)}, f32[272,128]{1,0:T(8,128)S(1)}, ...), condition=%wide.region_2.3_spmd.clone, body=%wide.region_1.2_spmd.clone.sunk | while | flops 591939 | bytes 1405943 | solution.py:51
  144.2 0.2 fusion.52
  145.7 0.2 fusion.52
  147.1 0.2 fusion.52
  148.6 0.2 fusion.52
  148.8 3.1 %collective-permute-start.3 = (f32[2,3,128]{2,0,1:T(2,128)S(1)}, f32[2,3,128]{2,0,1:T(2,128)S(1)}, u32[]{:S(2)}, u32[]{:S(2)}) collective-permute-start(f32[2,3,128]{2,0,1:T(2,128)S(1)} %slice.73), channel_id=1, source_target_pairs={{2,0},{4,2},{6,4},{8,6},{10,8},{12,10},{14,12},{3,1},{5,3},{7,5},{... | collective-permute-start | bytes 9224 | tf_op jit(solution)/shard_map/ppermute | solution.py:13
  151.9 2.7 %convert_element_type.14 = f32[272,4096]{1,0:T(8,128)} convert(bf16[272,4096]{1,0:T(8,128)(2,1)S(1)} %copy-done) | non-fusion elementwise | flops 1114112 | bytes 6684672 | tf_op jit(solution)/shard_map/convert_element_type | solution.py:90
  154.6 3.0 %gather_fusion.1 = f32[16,4096]{1,0:T(8,128)S(1)} fusion(f32[272,4096]{1,0:T(8,128)} %convert_element_type.14, s32[1024]{0:T(1024)S(1)} %pad_clamp_fusion), kind=kCustom, calls=%fused_computation.1.clone | custom fusion | bytes 524352 | tf_op jit(solution)/shard_map/jit(_take)/gather | solution.py:94
  157.8 4.1 %all_gather.8 = bf16[272,3,256]{2,0,1:T(8,128)(2,1)S(1)} all-gather(bf16[272,3,128]{2,0,1:T(8,128)(2,1)S(1)} %fusion.37), channel_id=1, replica_groups=mesh['rep'=2,'seq'=8,'grp'=2] {'grp'}, dimensions={2}, use_global_device_ids=true | all-gather | bytes 626688 | tf_op jit(solution)/shard_map/all_gather | solution.py:85
  162.0 7.0 %multiply_reduce_fusion = (f32[272]{0:T(512)S(1)}, f32[272,4096]{1,0:T(8,128)}) fusion(bf16[272,4096]{1,0:T(8,128)(2,1)S(1)} %copy-done, bf16[272,3,256]{2,0,1:T(8,128)(2,1)S(1)} %all_gather.8, bf16[3,256,4096]{2,1,0:T(8,128)(2,1)} %all-gather.2.cloned.1.call-done), kind=kOutput, calls=%fused_computation.51 | convolution fusion | flops 1714618112 | bytes 13395008 | tf_op jit(solution)/shard_map/tfc,fcd->td/dot_general | solution.py:87
  169.0 3.0 %gather_fusion = f32[16,4096]{1,0:T(8,128)S(1)} fusion(f32[272,4096]{1,0:T(8,128)} %get-tuple-element.361, s32[1024]{0:T(1024)S(1)} %pad_clamp_fusion), kind=kCustom, calls=%fused_computation.clone | custom fusion | bytes 524352 | tf_op jit(solution)/shard_map/jit(_take)/gather | solution.py:93
  172.0 0.2 fusion.41
  172.2 2.5 %all-reduce = (f32[272]{0:T(512)S(1)}, f32[16]{0:T(128)S(1)}) all-reduce(f32[272]{0:T(512)S(1)} %get-tuple-element.360, f32[16]{0:T(128)S(1)} %fusion.41), channel_id=1, replica_groups=mesh['rep'=2,'seq'=8,'grp'=2] {'grp'}, use_global_device_ids=true, to_apply=%region_6.7 | all-reduce | flops 288 | bytes 2304 | tf_op jit(solution)/shard_map/psum | solution.py:97
  174.7 0.6 broadcast_multiply_fusion
  175.3 0.5 broadcast_multiply_fusion.1
  (90 shorter events, 5.5 us)
Async XLA Ops:
  7.2 100.9 %all-gather.2.cloned.1.call-start = ((), (), s32[]{:S(2)}) async-start(), calls=%async_computation.1 | async-start | bytes 7077888 | tf_op jit(solution)/shard_map/all_gather | solution.py:63
  7.9 120.0 %copy-start.3 = (f32[3,3,128]{2,1,0:T(4,128)S(1)}, f32[3,3,128]{2,1,0:T(4,128)}, u32[]{:S(2)}) copy-start(f32[3,3,128]{2,1,0:T(4,128)} %param.15) | copy-start | bytes 13828
  7.9 123.7 %copy-start.1 = (bf16[272,128]{1,0:T(8,128)(2,1)S(1)}, bf16[272,128]{1,0:T(8,128)(2,1)}, u32[]{:S(2)}) copy-start(bf16[272,128]{1,0:T(8,128)(2,1)} %param.17) | copy-start | bytes 208900
  7.9 125.9 %copy-start.5 = (s32[16]{0:T(128)S(1)}, s32[16]{0:T(128)}, u32[]{:S(2)}) copy-start(s32[16]{0:T(128)} %param.18) | copy-start | bytes 196
  7.9 126.0 %copy-start.4 = (f32[8,128]{1,0:T(8,128)S(1)}, f32[8,128]{1,0:T(8,128)}, u32[]{:S(2)}) copy-start(f32[8,128]{1,0:T(8,128)} %param.16) | copy-start | bytes 12292
  7.9 116.2 %reduce-scatter.2.cloned.1.call-start = ((), (), s32[]{:S(2)}) async-start(), calls=%async_computation.2 | async-start | bytes 1253376 | tf_op jit(solution)/shard_map/reduce_scatter | solution.py:66
  124.9 5.2 %collective-permute-start = (f32[2,3,128]{2,0,1:T(2,128)S(1)}, f32[2,3,128]{2,0,1:T(2,128)S(1)}, u32[]{:S(2)}, u32[]{:S(2)}) collective-permute-start(f32[2,3,128]{2,0,1:T(2,128)S(1)} %slice.65), channel_id=1, source_target_pairs={{0,2},{2,4},{4,6},{6,8},{8,10},{10,12},{12,14},{1,3},{3,5},{5,7},{... | collective-permute-start | bytes 9224 | tf_op jit(solution)/shard_map/ppermute | solution.py:13
  131.7 5.5 %collective-permute-start.2 = (f32[127,128]{1,0:T(8,128)S(1)}, f32[127,128]{1,0:T(8,128)S(1)}, u32[]{:S(2)}, u32[]{:S(2)}) collective-permute-start(f32[127,128]{1,0:T(8,128)S(1)} %slice.72), channel_id=1, source_target_pairs={{2,0},{4,2},{6,4},{8,6},{10,8},{12,10},{14,12},{3,1},{5,3},{7,5},{... | collective-permute-start | bytes 195080 | tf_op jit(solution)/shard_map/ppermute | solution.py:13
  134.0 8.9 %collective-permute-start.1 = (f32[127,128]{1,0:T(8,128)S(1)}, f32[127,128]{1,0:T(8,128)S(1)}, u32[]{:S(2)}, u32[]{:S(2)}) collective-permute-start(f32[127,128]{1,0:T(8,128)S(1)} %slice.70), channel_id=1, source_target_pairs={{0,2},{2,4},{4,6},{6,8},{8,10},{10,12},{12,14},{1,3},{3,5},{5,7},{... | collective-permute-start | bytes 195080 | tf_op jit(solution)/shard_map/ppermute | solution.py:13
  143.0 9.0 %copy-start = (bf16[272,4096]{1,0:T(8,128)(2,1)S(1)}, bf16[272,4096]{1,0:T(8,128)(2,1)}, u32[]{:S(2)}) copy-start(bf16[272,4096]{1,0:T(8,128)(2,1)} %param.13) | copy-start | bytes 6684676
  148.8 8.8 %collective-permute-start.3 = (f32[2,3,128]{2,0,1:T(2,128)S(1)}, f32[2,3,128]{2,0,1:T(2,128)S(1)}, u32[]{:S(2)}, u32[]{:S(2)}) collective-permute-start(f32[2,3,128]{2,0,1:T(2,128)S(1)} %slice.73), channel_id=1, source_target_pairs={{2,0},{4,2},{6,4},{8,6},{10,8},{12,10},{14,12},{3,1},{5,3},{7,5},{... | collective-permute-start | bytes 9224 | tf_op jit(solution)/shard_map/ppermute | solution.py:13
  162.0 10.0 %copy-start.2 = (bf16[16,4096]{1,0:T(8,128)(2,1)S(1)}, bf16[16,4096]{1,0:T(8,128)(2,1)}, u32[]{:S(2)}) copy-start(bf16[16,4096]{1,0:T(8,128)(2,1)} %param.19) | copy-start | bytes 393220
Sparse Core Ops, SparseCore 0:
  10.2 97.8 all-gather.1
  114.6 9.5 reduce-scatter.1
where the time goes:
time: 183 us
  waiting for transfers between devices  113 us (62%)
  between operations  14.3 us (8%)
  matrix products  13.3 us (7%)
  other arithmetic  11.7 us (6%)
  starting transfers between devices  11.5 us (6%)
  local copies, waits for them, and re-layouts  7.86 us (4%)
  blocking collectives  6.62 us (4%)
  loops' own time  4.69 us (3%)
    all_gather x1, waiting for transfers between devices, per_device(): lax.all_gather(proj, 'seq', axis=1, tiled=True)  100 us
    ppermute x4, starting transfers between devices, shifted(): return lax.ppermute(block, axis, route)  11.4 us
    reduce_scatter x1, waiting for transfers between devices, per_device(): lax.psum_scatter(partial_feature, 'grp', scatter_dimension=2, tiled=True)  9.68 us
    dot_general x1, matrix products, per_device(): jnp.einsum('tfc,fcd->td', all_channels, panels_again, preferred_element_t...  7 us
    dot_general x1, matrix products, per_device(): jnp.einsum('td,fcd->tfc', hidden, lax.all_gather(proj, 'seq', axis=1, til...  6.32 us
    add x32, other arithmetic, accumulate(): summed + lax.dynamic_index_in_dim(per_channel, offset, 0, keepdims=False)...  5.8 us
    another operation x2, loops' own time, long_filter(): lax.fori_loop(0, filter_span // 8, accumulate, jnp.zeros((row_count, exte...  4.69 us
    all_gather x1, blocking collectives, per_device(): all_channels = lax.all_gather(back_feature, 'grp', axis=2, tiled=True)  4.13 us
  transfers between devices with their start and end apart: 6, of which 3 were waited for; matrix products, arithmetic and copies ran while one was open for 5% of the time, Pallas kernels for 0%

commit v1 on v0

--- a/solution.py
+++ b/solution.py
@@ -5,6 +5,24 @@
 
 D = 8192
 GROUP = 16
+
+
+def collect(shard, axis, dim):
+    ways, here, step = (lax.axis_size(axis), lax.axis_index(axis), shard.shape[dim])
+    shape = [n * ways if d == dim else n for d, n in enumerate(shard.shape)]
+    full = lax.dynamic_update_slice_in_dim(
+        jnp.zeros(shape, shard.dtype), shard, here * step, axis=dim
+    )
+    going_up = going_down = shard
+    for far in range(1, ways // 2 + 1):
+        going_up = lax.ppermute(going_up, axis, [(d, (d + 1) % ways) for d in range(ways)])
+        full = lax.dynamic_update_slice_in_dim(full, going_up, (here - far) % ways * step, axis=dim)
+        if 2 * far < ways:
+            going_down = lax.ppermute(going_down, axis, [(d, (d - 1) % ways) for d in range(ways)])
+            full = lax.dynamic_update_slice_in_dim(
+                full, going_down, (here + far) % ways * step, axis=dim
+            )
+    return full
 
 
 def shifted(block, axis, distance):
@@ -58,10 +76,7 @@
     tap_count = short_taps.shape[0]
     filter_span = filters.shape[1]
     partial_feature = jnp.einsum(
-        "td,fcd->tfc",
-        hidden,
-        lax.all_gather(proj, "seq", axis=1, tiled=True),
-        preferred_element_type=jnp.float32,
+        "td,fcd->tfc", hidden, collect(proj, "seq", 1), preferred_element_type=jnp.float32
     )
     feature = lax.psum_scatter(partial_feature, "grp", scatter_dimension=2, tiled=True)
     short_rim = shifted(feature[row_count - tap_count + 1 :], "seq", 1)

time: 183 us -> 263 us (1.44); the launches traced: 183 us -> 259 us
  local copies, waits for them, and re-layouts: 7.86 us -> 42.9 us
  waiting for transfers between devices: 113 us -> 141 us
  starting transfers between devices: 11.5 us -> 23.9 us
  matrix products: 13.3 us -> 9.73 us
    ppermute x0 -> x7, waiting for transfers between devices: none -> 109 us  [the longest x4 108 us: collect(): lax.ppermute(going_up, axis, [(d, (d + 1) % ways) for d in range(ways)])]
    all_gather x1, waiting for transfers between devices: 100 us -> 15.3 us  [per_device(): panels_again = lax.all_gather(proj, 'seq', axis=1, tiled=True)]
    mul x32, local copies, waits for them, and re-layouts: 0.99 us -> 31.8 us  [accumulate(): lax.dynamic_index_in_dim(per_channel, offset, 0, keepdims=False) * section]
    ppermute x0 -> x7, starting transfers between devices: none -> 8.92 us  [the longest x4 7.76 us: collect(): lax.ppermute(going_up, axis, [(d, (d + 1) % ways) for d in range(ways)])]
    ppermute x4, starting transfers between devices: 11.4 us -> 14.9 us  [shifted(): return lax.ppermute(block, axis, route)]
    dot_general x1, matrix products: 6.32 us -> 2.86 us  [per_device(): jnp.einsum('td,fcd->tfc', hidden, collect(proj, 'seq', 1), preferred_elem...]
    dynamic_update_slice x0 -> x8, local copies, waits for them, and re-layouts: none -> 2.81 us  [the longest x4 1.4 us: collect(): lax.dynamic_update_slice_in_dim(full, going_up, (here - far) % ways * ste...]
    ppermute x4, waiting for transfers between devices: 2.14 us -> 4.86 us  [shifted(): return lax.ppermute(block, axis, route)]
  transfers between devices with their start and end apart: 6 -> 13, of which waited for: 3 -> 12; matrix products, arithmetic and copies ran while one was open for 5% -> 20% of each run, Pallas kernels for 0% -> 0%
where the time goes in v1:
time: 263 us; the launch traced here: 259 us
  waiting for transfers between devices  141 us (54%)
  local copies, waits for them, and re-layouts  42.9 us (16%)
  starting transfers between devices  23.9 us (9%)
  between operations  15.8 us (6%)
  other arithmetic  13 us (5%)
  matrix products  9.73 us (4%)
  blocking collectives  8.67 us (3%)
  loops' own time  3.62 us (1%)
    ppermute x4, waiting for transfers between devices, collect(): lax.ppermute(going_up, axis, [(d, (d + 1) % ways) for d in range(ways)])  108 us
    mul x32, local copies, waits for them, and re-layouts, accumulate(): lax.dynamic_index_in_dim(per_channel, offset, 0, keepdims=False) * section  31.8 us
    all_gather x1, waiting for transfers between devices, per_device(): panels_again = lax.all_gather(proj, 'seq', axis=1, tiled=True)  15.3 us
    ppermute x4, starting transfers between devices, shifted(): return lax.ppermute(block, axis, route)  14.9 us
    reduce_scatter x1, waiting for transfers between devices, per_device(): lax.psum_scatter(partial_feature, 'grp', scatter_dimension=2, tiled=True)  11.2 us
    ppermute x4, starting transfers between devices, collect(): lax.ppermute(going_up, axis, [(d, (d + 1) % ways) for d in range(ways)])  7.76 us
    dot_general x1, matrix products, per_device(): jnp.einsum('tfc,fcd->td', all_channels, panels_again, preferred_element_t...  6.87 us
    add x32, other arithmetic, accumulate(): summed + lax.dynamic_index_in_dim(per_channel, offset, 0, keepdims=False)...  5.79 us
  transfers between devices with their start and end apart: 13, of which 12 were waited for; matrix products, arithmetic and copies ran while one was open for 20% of the time, Pallas kernels for 0%

profile of v1, /device:TPU:9, one launch (start us, length us, event | category | flops | bytes accessed | tf_op | source)
XLA Modules:
  0.0 258.9 jit_solution(16569166137006766940)
XLA Ops:
  8.1 1.3 collective-permute-start
  9.3 1.2 collective-permute-start.1
  11.3 31.3 %collective-permute-done = bf16[3,32,4096]{2,1,0:T(8,128)(2,1)} collective-permute-done((bf16[3,32,4096]{2,1,0:T(8,128)(2,1)}, bf16[3,32,4096]{2,1,0:T(8,128)(2,1)}, u32[]{:S(2)}, u32[]{:S(2)}) %collective-permute-start) | collective-permute-done | bytes 786464 | tf_op jit(solution)/shard_map/ppermute | solution.py:18
  42.7 2.2 collective-permute-start.2
  45.6 1.2 constant_dynamic-update-slice_fusion.6
  46.8 1.2 constant_dynamic-update-slice_fusion.5
  48.1 29.4 %collective-permute-done.2 = bf16[3,32,4096]{2,1,0:T(8,128)(2,1)S(1)} collective-permute-done((bf16[3,32,4096]{2,1,0:T(8,128)(2,1)}, bf16[3,32,4096]{2,1,0:T(8,128)(2,1)S(1)}, u32[]{:S(2)}, u32[]{:S(2)}) %collective-permute-start.2) | collective-permute-done | bytes 786464 | tf_op jit(solution)/shard_map/ppermute | solution.py:18
  77.5 2.1 collective-permute-start.4
  80.3 31.8 %collective-permute-done.4 = bf16[3,32,4096]{2,1,0:T(8,128)(2,1)S(1)} collective-permute-done((bf16[3,32,4096]{2,1,0:T(8,128)(2,1)S(1)}, bf16[3,32,4096]{2,1,0:T(8,128)(2,1)S(1)}, u32[]{:S(2)}, u32[]{:S(2)}) %collective-permute-start.4) | collective-permute-done | bytes 786464 | tf_op jit(solution)/shard_map/ppermute | solution.py:18
  112.1 2.2 collective-permute-start.6
  114.8 15.1 %collective-permute-done.6 = bf16[3,32,4096]{2,1,0:T(8,128)(2,1)S(1)} collective-permute-done((bf16[3,32,4096]{2,1,0:T(8,128)(2,1)S(1)}, bf16[3,32,4096]{2,1,0:T(8,128)(2,1)S(1)}, u32[]{:S(2)}, u32[]{:S(2)}) %collective-permute-start.6) | collective-permute-done | bytes 786464 | tf_op jit(solution)/shard_map/ppermute | solution.py:18
  130.1 2.9 %fusion.32 = f32[272,3,256]{2,0,1:T(8,128)} fusion(bf16[3,256,4096]{2,1,0:T(8,128)(2,1)S(1)} %constant_dynamic-update-slice_fusion, bf16[272,4096]{1,0:T(8,128)(2,1)S(1)} %copy-done), kind=kOutput, calls=%fused_computation.54 | convolution fusion | flops 1711276032 | bytes 9355264 | tf_op jit(solution)/shard_map/td,fcd->tfc/dot_general | solution.py:78
  133.5 11.2 %reduce-scatter.2.cloned.1.call-done = f32[272,3,128]{2,0,1:T(8,128)} async-done(((f32[272,3,256]{2,0,1:T(8,128)}), f32[272,3,128]{2,0,1:T(8,128)}) %reduce-scatter.2.cloned.1.call-update) | async-done | bytes 417808 | tf_op jit(solution)/shard_map/reduce_scatter | solution.py:81
  145.4 3.1 %collective-permute-start.7 = (f32[2,3,128]{2,0,1:T(2,128)S(1)}, f32[2,3,128]{2,0,1:T(2,128)S(1)}, u32[]{:S(2)}, u32[]{:S(2)}) collective-permute-start(f32[2,3,128]{2,0,1:T(2,128)S(1)} %slice.65), channel_id=1, source_target_pairs={{0,2},{2,4},{4,6},{6,8},{8,10},{10,12},{12,14},{1,3},{3,5},{5,7},{... | collective-permute-start | bytes 9224 | tf_op jit(solution)/shard_map/ppermute | solution.py:31
  148.6 2.2 collective-permute-done.7
  150.8 1.5 fusion.38
  152.3 2.5 collective-permute-start.8
  156.1 3.7 %collective-permute-start.9 = (f32[127,128]{1,0:T(8,128)S(1)}, f32[127,128]{1,0:T(8,128)S(1)}, u32[]{:S(2)}, u32[]{:S(2)}) collective-permute-start(f32[127,128]{1,0:T(8,128)S(1)} %slice.72), channel_id=1, source_target_pairs={{2,0},{4,2},{6,4},{8,6},{10,8},{12,10},{14,12},{3,1},{5,3},{7,5},{... | collective-permute-start | bytes 195080 | tf_op jit(solution)/shard_map/ppermute | solution.py:31
  160.9 2.4 collective-permute-done.9
  163.3 20.7 %while.33 = (s32[]{:T(128)}, f32[272,128]{1,0:T(8,128)S(1)}, f32[128,128]{1,0:T(8,128)}, f32[399,128]{1,0:T(8,128)S(1)}, s32[]{:T(128)}, /*index=5*/s32[]{:T(128...) while((s32[]{:T(128)}, f32[272,128]{1,0:T(8,128)S(1)}, ...), condition=%wide.region_2.3_spmd.clone, body=%wide.region_1.2_spmd.clone.sunk | while | flops 591939 | bytes 1405943 | solution.py:69
  167.3 1.0 fusion.54
  172.5 1.0 fusion.54
  184.1 20.5 %while.34 = (s32[]{:T(128)}, f32[272,128]{1,0:T(8,128)S(1)}, f32[128,128]{1,0:T(8,128)}, f32[399,128]{1,0:T(8,128)S(1)}, s32[]{:T(128)}, /*index=5*/s32[]{:T(128...) while((s32[]{:T(128)}, f32[272,128]{1,0:T(8,128)S(1)}, ...), condition=%wide.region_4.5_spmd.clone, body=%wide.region_3.4_spmd.clone.sunk | while | flops 591923 | bytes 1405823 | solution.py:69
  188.0 1.0 fusion.56
  204.7 5.7 %collective-permute-start.10 = (f32[2,3,128]{2,0,1:T(2,128)S(1)}, f32[2,3,128]{2,0,1:T(2,128)S(1)}, u32[]{:S(2)}, u32[]{:S(2)}) collective-permute-start(f32[2,3,128]{2,0,1:T(2,128)S(1)} %slice.73), channel_id=1, source_target_pairs={{2,0},{4,2},{6,4},{8,6},{10,8},{12,10},{14,12},{3,1},{5,3},{7,5},{... | collective-permute-start | bytes 9224 | tf_op jit(solution)/shard_map/ppermute | solution.py:31
  210.4 2.7 %convert_element_type.14 = f32[272,4096]{1,0:T(8,128)} convert(bf16[272,4096]{1,0:T(8,128)(2,1)S(1)} %copy-done) | non-fusion elementwise | flops 1114112 | bytes 6684672 | tf_op jit(solution)/shard_map/convert_element_type | solution.py:105
  213.0 3.0 %gather_fusion.1 = f32[16,4096]{1,0:T(8,128)S(1)} fusion(f32[272,4096]{1,0:T(8,128)} %convert_element_type.14, s32[1024]{0:T(1024)S(1)} %pad_clamp_fusion), kind=kCustom, calls=%fused_computation.1.clone | custom fusion | bytes 524352 | tf_op jit(solution)/shard_map/jit(_take)/gather | solution.py:109
  216.3 4.7 %all_gather.6 = bf16[272,3,256]{2,0,1:T(8,128)(2,1)S(1)} all-gather(bf16[272,3,128]{2,0,1:T(8,128)(2,1)S(1)} %fusion.40), channel_id=1, replica_groups=mesh['rep'=2,'seq'=8,'grp'=2] {'grp'}, dimensions={2}, use_global_device_ids=true | all-gather | bytes 626688 | tf_op jit(solution)/shard_map/all_gather | solution.py:100
  221.0 15.3 %all-gather.2.cloned.1.call-done = bf16[3,256,4096]{2,1,0:T(8,128)(2,1)} async-done(((bf16[3,32,4096]{2,1,0:T(8,128)(2,1)}), bf16[3,256,4096]{2,1,0:T(8,128)(2,1)}) %all-gather.2.cloned.1.call-update) | async-done | bytes 6291472 | tf_op jit(solution)/shard_map/all_gather | solution.py:101
  236.2 6.9 %multiply_reduce_fusion = (f32[272]{0:T(512)S(1)}, f32[272,4096]{1,0:T(8,128)}) fusion(bf16[272,4096]{1,0:T(8,128)(2,1)S(1)} %copy-done, bf16[272,3,256]{2,0,1:T(8,128)(2,1)S(1)} %all_gather.6, bf16[3,256,4096]{2,1,0:T(8,128)(2,1)} %all-gather.2.cloned.1.call-done), kind=kOutput, calls=%fused_computation.51 | convolution fusion | flops 1714618112 | bytes 13395008 | tf_op jit(solution)/shard_map/tfc,fcd->td/dot_general | solution.py:102
  243.1 3.0 %gather_fusion = f32[16,4096]{1,0:T(8,128)S(1)} fusion(f32[272,4096]{1,0:T(8,128)} %get-tuple-element.361, s32[1024]{0:T(1024)S(1)} %pad_clamp_fusion), kind=kCustom, calls=%fused_computation.clone | custom fusion | bytes 524352 | tf_op jit(solution)/shard_map/jit(_take)/gather | solution.py:108
  246.4 4.0 %all-reduce = (f32[272]{0:T(512)S(1)}, f32[16]{0:T(128)S(1)}) all-reduce(f32[272]{0:T(512)S(1)} %get-tuple-element.360, f32[16]{0:T(128)S(1)} %fusion.44), channel_id=1, replica_groups=mesh['rep'=2,'seq'=8,'grp'=2] {'grp'}, use_global_device_ids=true, to_apply=%region_6.7 | all-reduce | flops 288 | bytes 2304 | tf_op jit(solution)/shard_map/psum | solution.py:112
  (119 shorter events, 42.9 us)
Async XLA Ops:
  8.0 3.2 %copy-start.1 = (bf16[3,32,4096]{2,1,0:T(8,128)(2,1)S(1)}, bf16[3,32,4096]{2,1,0:T(8,128)(2,1)}, u32[]{:S(2)}) copy-start(bf16[3,32,4096]{2,1,0:T(8,128)(2,1)} %param.14) | copy-start | bytes 2359300
  8.0 136.7 %reduce-scatter.2.cloned.1.call-start = ((), (), s32[]{:S(2)}) async-start(), calls=%async_computation.1 | async-start | bytes 1253376 | tf_op jit(solution)/shard_map/reduce_scatter | solution.py:81
  8.1 34.6 %collective-permute-start = (bf16[3,32,4096]{2,1,0:T(8,128)(2,1)}, bf16[3,32,4096]{2,1,0:T(8,128)(2,1)}, u32[]{:S(2)}, u32[]{:S(2)}) collective-permute-start(bf16[3,32,4096]{2,1,0:T(8,128)(2,1)} %param.14), channel_id=1, source_target_pairs={{0,2},{2,4},{4,6},{6,8},{8,10},{10,12},{12,14},{14,0},{1,3},{3,5},... | collective-permute-start | bytes 2359304 | tf_op jit(solution)/shard_map/ppermute | solution.py:18
  9.3 36.3 %collective-permute-start.1 = (bf16[3,32,4096]{2,1,0:T(8,128)(2,1)}, bf16[3,32,4096]{2,1,0:T(8,128)(2,1)}, u32[]{:S(2)}, u32[]{:S(2)}) collective-permute-start(bf16[3,32,4096]{2,1,0:T(8,128)(2,1)} %param.14), channel_id=1, source_target_pairs={{0,14},{2,0},{4,2},{6,4},{8,6},{10,8},{12,10},{14,12},{1,15},{3,1}... | collective-permute-start | bytes 2359304 | tf_op jit(solution)/shard_map/ppermute | solution.py:21
  11.3 118.8 %copy-start = (bf16[272,4096]{1,0:T(8,128)(2,1)S(1)}, bf16[272,4096]{1,0:T(8,128)(2,1)}, u32[]{:S(2)}) copy-start(bf16[272,4096]{1,0:T(8,128)(2,1)} %param.13) | copy-start | bytes 6684676
  42.7 34.8 %collective-permute-start.2 = (bf16[3,32,4096]{2,1,0:T(8,128)(2,1)}, bf16[3,32,4096]{2,1,0:T(8,128)(2,1)S(1)}, u32[]{:S(2)}, u32[]{:S(2)}) collective-permute-start(bf16[3,32,4096]{2,1,0:T(8,128)(2,1)} %collective-permute-done), channel_id=1, source_target_pairs={{0,2},{2,4},{4,6},{6,8},{8,10},{10,12},{12,14},{14,0},{1,3},{3,5},... | collective-permute-start | bytes 2359304 | tf_op jit(solution)/shard_map/ppermute | solution.py:18
  45.6 34.5 %collective-permute-start.3 = (bf16[3,32,4096]{2,1,0:T(8,128)(2,1)}, bf16[3,32,4096]{2,1,0:T(8,128)(2,1)S(1)}, u32[]{:S(2)}, u32[]{:S(2)}) collective-permute-start(bf16[3,32,4096]{2,1,0:T(8,128)(2,1)} %collective-permute-done.1), channel_id=1, source_target_pairs={{0,14},{2,0},{4,2},{6,4},{8,6},{10,8},{12,10},{14,12},{1,15},{3,1}... | collective-permute-start | bytes 2359304 | tf_op jit(solution)/shard_map/ppermute | solution.py:21
  77.5 34.6 %collective-permute-start.4 = (bf16[3,32,4096]{2,1,0:T(8,128)(2,1)S(1)}, bf16[3,32,4096]{2,1,0:T(8,128)(2,1)S(1)}, u32[]{:S(2)}, u32[]{:S(2)}) collective-permute-start(bf16[3,32,4096]{2,1,0:T(8,128)(2,1)S(1)} %collective-permute-done.2), channel_id=1, source_target_pairs={{0,2},{2,4},{4,6},{6,8},{8,10},{10,12},{12,14},{14,0},{1,3},{3,5},... | collective-permute-start | bytes 2359304 | tf_op jit(solution)/shard_map/ppermute | solution.py:18
  80.1 34.6 %collective-permute-start.5 = (bf16[3,32,4096]{2,1,0:T(8,128)(2,1)S(1)}, bf16[3,32,4096]{2,1,0:T(8,128)(2,1)S(1)}, u32[]{:S(2)}, u32[]{:S(2)}) collective-permute-start(bf16[3,32,4096]{2,1,0:T(8,128)(2,1)S(1)} %collective-permute-done.3), channel_id=1, source_target_pairs={{0,14},{2,0},{4,2},{6,4},{8,6},{10,8},{12,10},{14,12},{1,15},{3,1}... | collective-permute-start | bytes 2359304 | tf_op jit(solution)/shard_map/ppermute | solution.py:21
  112.1 17.8 %collective-permute-start.6 = (bf16[3,32,4096]{2,1,0:T(8,128)(2,1)S(1)}, bf16[3,32,4096]{2,1,0:T(8,128)(2,1)S(1)}, u32[]{:S(2)}, u32[]{:S(2)}) collective-permute-start(bf16[3,32,4096]{2,1,0:T(8,128)(2,1)S(1)} %collective-permute-done.4), channel_id=1, source_target_pairs={{0,2},{2,4},{4,6},{6,8},{8,10},{10,12},{12,14},{14,0},{1,3},{3,5},... | collective-permute-start | bytes 2359304 | tf_op jit(solution)/shard_map/ppermute | solution.py:18
  130.0 18.5 %copy-start.4 = (f32[3,3,128]{2,1,0:T(4,128)S(1)}, f32[3,3,128]{2,1,0:T(4,128)}, u32[]{:S(2)}) copy-start(f32[3,3,128]{2,1,0:T(4,128)} %param.15) | copy-start | bytes 13828
  130.0 22.2 %copy-start.2 = (bf16[272,128]{1,0:T(8,128)(2,1)S(1)}, bf16[272,128]{1,0:T(8,128)(2,1)}, u32[]{:S(2)}) copy-start(bf16[272,128]{1,0:T(8,128)(2,1)} %param.17) | copy-start | bytes 208900
  130.0 24.8 %copy-start.8 = (s32[16]{0:T(128)S(1)}, s32[16]{0:T(128)}, u32[]{:S(2)}) copy-start(s32[16]{0:T(128)} %param.18) | copy-start | bytes 196
  130.0 25.4 %copy-start.5 = (f32[8,128]{1,0:T(8,128)S(1)}, f32[8,128]{1,0:T(8,128)}, u32[]{:S(2)}) copy-start(f32[8,128]{1,0:T(8,128)} %param.16) | copy-start | bytes 12292
  132.9 103.3 %all-gather.2.cloned.1.call-start = ((), (), s32[]{:S(2)}) async-start(), calls=%async_computation.2 | async-start | bytes 7077888 | tf_op jit(solution)/shard_map/all_gather | solution.py:101
  145.4 5.3 %collective-permute-start.7 = (f32[2,3,128]{2,0,1:T(2,128)S(1)}, f32[2,3,128]{2,0,1:T(2,128)S(1)}, u32[]{:S(2)}, u32[]{:S(2)}) collective-permute-start(f32[2,3,128]{2,0,1:T(2,128)S(1)} %slice.65), channel_id=1, source_target_pairs={{0,2},{2,4},{4,6},{6,8},{8,10},{10,12},{12,14},{1,3},{3,5},{5,7},{... | collective-permute-start | bytes 9224 | tf_op jit(solution)/shard_map/ppermute | solution.py:31
  152.3 7.8 %collective-permute-start.8 = (f32[127,128]{1,0:T(8,128)S(1)}, f32[127,128]{1,0:T(8,128)}, u32[]{:S(2)}, u32[]{:S(2)}) collective-permute-start(f32[127,128]{1,0:T(8,128)S(1)} %slice.70), channel_id=1, source_target_pairs={{0,2},{2,4},{4,6},{6,8},{8,10},{10,12},{12,14},{1,3},{3,5},{5,7},{... | collective-permute-start | bytes 195080 | tf_op jit(solution)/shard_map/ppermute | solution.py:31
  156.1 7.2 %collective-permute-start.9 = (f32[127,128]{1,0:T(8,128)S(1)}, f32[127,128]{1,0:T(8,128)S(1)}, u32[]{:S(2)}, u32[]{:S(2)}) collective-permute-start(f32[127,128]{1,0:T(8,128)S(1)} %slice.72), channel_id=1, source_target_pairs={{2,0},{4,2},{6,4},{8,6},{10,8},{12,10},{14,12},{3,1},{5,3},{7,5},{... | collective-permute-start | bytes 195080 | tf_op jit(solution)/shard_map/ppermute | solution.py:31
  184.0 26.3 %copy-start.7 = (s32[16]{0:T(128)S(1)}, s32[16]{0:T(128)}, u32[]{:S(2)}) copy-start(s32[16]{0:T(128)} %get-tuple-element.336) | copy-start | bytes 196
  204.7 11.4 %collective-permute-start.10 = (f32[2,3,128]{2,0,1:T(2,128)S(1)}, f32[2,3,128]{2,0,1:T(2,128)S(1)}, u32[]{:S(2)}, u32[]{:S(2)}) collective-permute-start(f32[2,3,128]{2,0,1:T(2,128)S(1)} %slice.73), channel_id=1, source_target_pairs={{2,0},{4,2},{6,4},{8,6},{10,8},{12,10},{14,12},{3,1},{5,3},{7,5},{... | collective-permute-start | bytes 9224 | tf_op jit(solution)/shard_map/ppermute | solution.py:31
  221.0 25.2 %copy-start.3 = (bf16[16,4096]{1,0:T(8,128)(2,1)S(1)}, bf16[16,4096]{1,0:T(8,128)(2,1)}, u32[]{:S(2)}) copy-start(bf16[16,4096]{1,0:T(8,128)(2,1)} %param.19) | copy-start | bytes 393220
  221.0 25.2 %copy-start.6 = (pred[16]{0:T(512)(128)(4,1)S(1)}, pred[16]{0:T(512)(128)(4,1)}, u32[]{:S(2)}) copy-start(pred[16]{0:T(512)(128)(4,1)} %get-tuple-element.335) | copy-start | bytes 52
Sparse Core Ops, SparseCore 0:
  133.1 11.6 reduce-scatter.1
Sparse Core Ops, SparseCore 1:
  135.8 100.4 all-gather.1
